TPU v7x, 32 devices: a whole 2x2x4 slice. The times are simulated.
32 devices in a mesh: tok: 8 (over y, x, core), own: 4 (over z).
Axes of the slice: x: 2, y: 2, z: 4, core: 2. Of those that a mesh axis runs over, the one named last changes fastest.
Arguments:
- expert_ids: int32 [5, 8, 262144], P(None, None, ('tok', 'own')), may hold values from 0 to 383, as said below
- shard_length: int32 [32], P(('tok', 'own')), may hold values from 2048 to 8192
Outputs:
- lift: float32 [4, 384, 384], P(None, 'own')
Inputs may be any that keep to these rules, and one draw needn't show every extreme that they name: For each layer and token slot, expert_ids names 8 different experts.
All inputs are finite; a program needn't handle non-finite values.
Results may differ from a plain program's by a relative error of at most 0.0003.
Values sent between devices are 32-bit elements; how exact they have to be, the bound alone decides.
A program may use at most 64 MiB of HBM per device.

v0:
```python
import jax
import jax.numpy as jnp
from jax import lax
from jax.sharding import PartitionSpec as P

E = 384


def shards(expert_ids, shard_length):
    layers, chosen, slots = expert_ids.shape
    block = min(slots, 512 * max(1, slots // 8192))
    steps = slots // block
    experts = E
    limit = shard_length[0]
    columns = lax.broadcasted_iota(jnp.int32, (1, 1, experts), 2)

    def one_block(index, carry):
        counts, tiles = carry
        start = index * block
        piece = lax.dynamic_slice_in_dim(expert_ids, start, block, 2)
        rows = start + lax.broadcasted_iota(jnp.int32, (1, block, 1), 1)
        alive = (rows < limit).astype(jnp.bfloat16)
        hot = jnp.zeros((layers, block, experts), jnp.bfloat16)
        for slot in range(chosen):
            hot = hot + (piece[:, slot, :, None] == columns).astype(jnp.bfloat16)
        hot = hot * alive
        counts = counts + jnp.sum(hot, axis=1, dtype=jnp.float32)
        tiles = tiles + jnp.einsum(
            "ltx,lty->lxy", hot[:-1], hot[1:], preferred_element_type=jnp.float32
        )
        return (counts, tiles)

    begin = (
        jnp.zeros((layers, experts), jnp.float32),
        jnp.zeros((layers - 1, experts, experts), jnp.float32),
    )
    counts, tiles = lax.fori_loop(0, steps, one_block, begin)
    counts, total = lax.psum((counts, limit.astype(jnp.float32)), ("tok", "own"))
    owners = lax.axis_size("own")
    share = experts // owners
    partial_rows = lax.psum_scatter(tiles, "own", scatter_dimension=1, tiled=True)
    mine = lax.psum(partial_rows, "tok")
    first = lax.dynamic_slice_in_dim(counts[:-1], lax.axis_index("own") * share, share, 1)
    product = first[:, :, None] * counts[1:, None, :]
    return mine * total / jnp.maximum(product, 1.0)


def solution(mesh):
    placed = (P(None, None, ("tok", "own")), P(("tok", "own")))
    return jax.shard_map(
        shards, mesh=mesh, in_specs=placed, out_specs=P(None, "own", None), check_vma=False
    )
```

profile of v0, /device:TPU:0, one launch (start us, length us, event | category | flops | bytes accessed | tf_op | source)
XLA Modules:
  0.0 295.4 jit_solution(4349476198829206356)
XLA Ops:
  6.5 170.0 %while.17 = (s32[]{:T(128)}, f32[5,384]{1,0:T(8,128)S(1)}, f32[4,384,384]{2,1,0:T(8,128)}, s32[5,8,8192]{2,1,0:T(8,128)}, s32[]{:T(128)}, /*index=5*/s32[]{:T(12...) while((s32[]{:T(128)}, f32[5,384]{1,0:T(8,128)S(1)}, ...), condition=%wide.region_2.0_spmd.clone.clone, body=%wide.region_0.0_spmd.clone.clone.sunk | while | flops 640552320 | bytes 10666322 | solution.py:37
  8.7 4.0 %convert_reduce_fusion.2 = (f32[5,384]{1,0:T(8,128)S(1)}, bf16[5,512,384]{2,1,0:T(8,128)(2,1)S(1)}) fusion(bf16[512]{0:T(512)(128)(2,1)S(1)} %fusion.31, s32[5,512]{1,0:T(8,128)S(1)} %get-tuple-element.268, s32[5,512]{1,0:T(8,128)S(1)} %get-tuple-element.269, s32[5,512]{1,0:T(8,128)S(1)} %get-tuple-element.272, s32[5,512]{1,0:T(8,128)S(1)} %get-tuple-element.273, ...), kind=kLoop, calls=%fused_computation.9.clone.1 | loop fusion | flops 35387520 | bytes 2056704 | tf_op jit(solution)/shard_map/while/body/eval_jaxpr/reduce_sum | solution.py:27
  17.5 4.0 %convert_reduce_fusion.2 = (f32[5,384]{1,0:T(8,128)S(1)}, bf16[5,512,384]{2,1,0:T(8,128)(2,1)S(1)}) fusion(bf16[512]{0:T(512)(128)(2,1)S(1)} %fusion.31, s32[5,512]{1,0:T(8,128)S(1)} %get-tuple-element.268, s32[5,512]{1,0:T(8,128)S(1)} %get-tuple-element.269, s32[5,512]{1,0:T(8,128)S(1)} %get-tuple-element.272, s32[5,512]{1,0:T(8,128)S(1)} %get-tuple-element.273, ...), kind=kLoop, calls=%fused_computation.9.clone.1 | loop fusion | flops 35387520 | bytes 2056704 | tf_op jit(solution)/shard_map/while/body/eval_jaxpr/reduce_sum | solution.py:27
  21.6 4.2 %select_add_fusion.5 = f32[4,384,384]{2,1,0:T(8,128)} fusion(f32[4,384,384]{2,1,0:T(8,128)} %get-tuple-element.302, bf16[5,512,384]{2,1,0:T(8,128)(2,1)S(1)} %get-tuple-element.283, pred[]{:T(512)S(6)} %compare.3), kind=kOutput, calls=%fused_computation.18.clone.1 | convolution fusion | flops 605159424 | bytes 8257537 | tf_op jit(solution)/shard_map/while/body/eval_jaxpr/ltx,lty->lxy/dot_general | solution.py:28
  28.3 4.0 %convert_reduce_fusion.2 = (f32[5,384]{1,0:T(8,128)S(1)}, bf16[5,512,384]{2,1,0:T(8,128)(2,1)S(1)}) fusion(bf16[512]{0:T(512)(128)(2,1)S(1)} %fusion.31, s32[5,512]{1,0:T(8,128)S(1)} %get-tuple-element.268, s32[5,512]{1,0:T(8,128)S(1)} %get-tuple-element.269, s32[5,512]{1,0:T(8,128)S(1)} %get-tuple-element.272, s32[5,512]{1,0:T(8,128)S(1)} %get-tuple-element.273, ...), kind=kLoop, calls=%fused_computation.9.clone.1 | loop fusion | flops 35387520 | bytes 2056704 | tf_op jit(solution)/shard_map/while/body/eval_jaxpr/reduce_sum | solution.py:27
  32.4 4.2 %select_add_fusion.5 = f32[4,384,384]{2,1,0:T(8,128)} fusion(f32[4,384,384]{2,1,0:T(8,128)} %get-tuple-element.302, bf16[5,512,384]{2,1,0:T(8,128)(2,1)S(1)} %get-tuple-element.283, pred[]{:T(512)S(6)} %compare.3), kind=kOutput, calls=%fused_computation.18.clone.1 | convolution fusion | flops 605159424 | bytes 8257537 | tf_op jit(solution)/shard_map/while/body/eval_jaxpr/ltx,lty->lxy/dot_general | solution.py:28
  39.1 4.0 %convert_reduce_fusion.2 = (f32[5,384]{1,0:T(8,128)S(1)}, bf16[5,512,384]{2,1,0:T(8,128)(2,1)S(1)}) fusion(bf16[512]{0:T(512)(128)(2,1)S(1)} %fusion.31, s32[5,512]{1,0:T(8,128)S(1)} %get-tuple-element.268, s32[5,512]{1,0:T(8,128)S(1)} %get-tuple-element.269, s32[5,512]{1,0:T(8,128)S(1)} %get-tuple-element.272, s32[5,512]{1,0:T(8,128)S(1)} %get-tuple-element.273, ...), kind=kLoop, calls=%fused_computation.9.clone.1 | loop fusion | flops 35387520 | bytes 2056704 | tf_op jit(solution)/shard_map/while/body/eval_jaxpr/reduce_sum | solution.py:27
  43.1 4.2 %select_add_fusion.5 = f32[4,384,384]{2,1,0:T(8,128)} fusion(f32[4,384,384]{2,1,0:T(8,128)} %get-tuple-element.302, bf16[5,512,384]{2,1,0:T(8,128)(2,1)S(1)} %get-tuple-element.283, pred[]{:T(512)S(6)} %compare.3), kind=kOutput, calls=%fused_computation.18.clone.1 | convolution fusion | flops 605159424 | bytes 8257537 | tf_op jit(solution)/shard_map/while/body/eval_jaxpr/ltx,lty->lxy/dot_general | solution.py:28
  49.8 4.0 %convert_reduce_fusion.2 = (f32[5,384]{1,0:T(8,128)S(1)}, bf16[5,512,384]{2,1,0:T(8,128)(2,1)S(1)}) fusion(bf16[512]{0:T(512)(128)(2,1)S(1)} %fusion.31, s32[5,512]{1,0:T(8,128)S(1)} %get-tuple-element.268, s32[5,512]{1,0:T(8,128)S(1)} %get-tuple-element.269, s32[5,512]{1,0:T(8,128)S(1)} %get-tuple-element.272, s32[5,512]{1,0:T(8,128)S(1)} %get-tuple-element.273, ...), kind=kLoop, calls=%fused_computation.9.clone.1 | loop fusion | flops 35387520 | bytes 2056704 | tf_op jit(solution)/shard_map/while/body/eval_jaxpr/reduce_sum | solution.py:27
  53.9 4.2 %select_add_fusion.5 = f32[4,384,384]{2,1,0:T(8,128)} fusion(f32[4,384,384]{2,1,0:T(8,128)} %get-tuple-element.302, bf16[5,512,384]{2,1,0:T(8,128)(2,1)S(1)} %get-tuple-element.283, pred[]{:T(512)S(6)} %compare.3), kind=kOutput, calls=%fused_computation.18.clone.1 | convolution fusion | flops 605159424 | bytes 8257537 | tf_op jit(solution)/shard_map/while/body/eval_jaxpr/ltx,lty->lxy/dot_general | solution.py:28
  64.6 4.2 %select_add_fusion.5 = f32[4,384,384]{2,1,0:T(8,128)} fusion(f32[4,384,384]{2,1,0:T(8,128)} %get-tuple-element.302, bf16[5,512,384]{2,1,0:T(8,128)(2,1)S(1)} %get-tuple-element.283, pred[]{:T(512)S(6)} %compare.3), kind=kOutput, calls=%fused_computation.18.clone.1 | convolution fusion | flops 605159424 | bytes 8257537 | tf_op jit(solution)/shard_map/while/body/eval_jaxpr/ltx,lty->lxy/dot_general | solution.py:28
  75.3 4.2 %select_add_fusion.5 = f32[4,384,384]{2,1,0:T(8,128)} fusion(f32[4,384,384]{2,1,0:T(8,128)} %get-tuple-element.302, bf16[5,512,384]{2,1,0:T(8,128)(2,1)S(1)} %get-tuple-element.283, pred[]{:T(512)S(6)} %compare.3), kind=kOutput, calls=%fused_computation.18.clone.1 | convolution fusion | flops 605159424 | bytes 8257537 | tf_op jit(solution)/shard_map/while/body/eval_jaxpr/ltx,lty->lxy/dot_general | solution.py:28
  86.0 4.2 %select_add_fusion.5 = f32[4,384,384]{2,1,0:T(8,128)} fusion(f32[4,384,384]{2,1,0:T(8,128)} %get-tuple-element.302, bf16[5,512,384]{2,1,0:T(8,128)(2,1)S(1)} %get-tuple-element.283, pred[]{:T(512)S(6)} %compare.3), kind=kOutput, calls=%fused_computation.18.clone.1 | convolution fusion | flops 605159424 | bytes 8257537 | tf_op jit(solution)/shard_map/while/body/eval_jaxpr/ltx,lty->lxy/dot_general | solution.py:28
  96.5 4.2 %select_add_fusion.5 = f32[4,384,384]{2,1,0:T(8,128)} fusion(f32[4,384,384]{2,1,0:T(8,128)} %get-tuple-element.302, bf16[5,512,384]{2,1,0:T(8,128)(2,1)S(1)} %get-tuple-element.283, pred[]{:T(512)S(6)} %compare.3), kind=kOutput, calls=%fused_computation.18.clone.1 | convolution fusion | flops 605159424 | bytes 8257537 | tf_op jit(solution)/shard_map/while/body/eval_jaxpr/ltx,lty->lxy/dot_general | solution.py:28
  107.2 4.2 %select_add_fusion.5 = f32[4,384,384]{2,1,0:T(8,128)} fusion(f32[4,384,384]{2,1,0:T(8,128)} %get-tuple-element.302, bf16[5,512,384]{2,1,0:T(8,128)(2,1)S(1)} %get-tuple-element.283, pred[]{:T(512)S(6)} %compare.3), kind=kOutput, calls=%fused_computation.18.clone.1 | convolution fusion | flops 605159424 | bytes 8257537 | tf_op jit(solution)/shard_map/while/body/eval_jaxpr/ltx,lty->lxy/dot_general | solution.py:28
  118.0 4.2 %select_add_fusion.5 = f32[4,384,384]{2,1,0:T(8,128)} fusion(f32[4,384,384]{2,1,0:T(8,128)} %get-tuple-element.302, bf16[5,512,384]{2,1,0:T(8,128)(2,1)S(1)} %get-tuple-element.283, pred[]{:T(512)S(6)} %compare.3), kind=kOutput, calls=%fused_computation.18.clone.1 | convolution fusion | flops 605159424 | bytes 8257537 | tf_op jit(solution)/shard_map/while/body/eval_jaxpr/ltx,lty->lxy/dot_general | solution.py:28
  129.0 4.2 %select_add_fusion.5 = f32[4,384,384]{2,1,0:T(8,128)} fusion(f32[4,384,384]{2,1,0:T(8,128)} %get-tuple-element.302, bf16[5,512,384]{2,1,0:T(8,128)(2,1)S(1)} %get-tuple-element.283, pred[]{:T(512)S(6)} %compare.3), kind=kOutput, calls=%fused_computation.18.clone.1 | convolution fusion | flops 605159424 | bytes 8257537 | tf_op jit(solution)/shard_map/while/body/eval_jaxpr/ltx,lty->lxy/dot_general | solution.py:28
  140.0 4.2 %select_add_fusion.5 = f32[4,384,384]{2,1,0:T(8,128)} fusion(f32[4,384,384]{2,1,0:T(8,128)} %get-tuple-element.302, bf16[5,512,384]{2,1,0:T(8,128)(2,1)S(1)} %get-tuple-element.283, pred[]{:T(512)S(6)} %compare.3), kind=kOutput, calls=%fused_computation.18.clone.1 | convolution fusion | flops 605159424 | bytes 8257537 | tf_op jit(solution)/shard_map/while/body/eval_jaxpr/ltx,lty->lxy/dot_general | solution.py:28
  150.8 4.2 %select_add_fusion.5 = f32[4,384,384]{2,1,0:T(8,128)} fusion(f32[4,384,384]{2,1,0:T(8,128)} %get-tuple-element.302, bf16[5,512,384]{2,1,0:T(8,128)(2,1)S(1)} %get-tuple-element.283, pred[]{:T(512)S(6)} %compare.3), kind=kOutput, calls=%fused_computation.18.clone.1 | convolution fusion | flops 605159424 | bytes 8257537 | tf_op jit(solution)/shard_map/while/body/eval_jaxpr/ltx,lty->lxy/dot_general | solution.py:28
  161.6 4.2 %select_add_fusion.5 = f32[4,384,384]{2,1,0:T(8,128)} fusion(f32[4,384,384]{2,1,0:T(8,128)} %get-tuple-element.302, bf16[5,512,384]{2,1,0:T(8,128)(2,1)S(1)} %get-tuple-element.283, pred[]{:T(512)S(6)} %compare.3), kind=kOutput, calls=%fused_computation.18.clone.1 | convolution fusion | flops 605159424 | bytes 8257537 | tf_op jit(solution)/shard_map/while/body/eval_jaxpr/ltx,lty->lxy/dot_general | solution.py:28
  172.3 4.2 %select_add_fusion.5 = f32[4,384,384]{2,1,0:T(8,128)} fusion(f32[4,384,384]{2,1,0:T(8,128)} %get-tuple-element.302, bf16[5,512,384]{2,1,0:T(8,128)(2,1)S(1)} %get-tuple-element.283, pred[]{:T(512)S(6)} %compare.3), kind=kOutput, calls=%fused_computation.18.clone.1 | convolution fusion | flops 605159424 | bytes 8257537 | tf_op jit(solution)/shard_map/while/body/eval_jaxpr/ltx,lty->lxy/dot_general | solution.py:28
  177.3 44.8 %all-reduce = (f32[5,384]{1,0:T(8,128)S(1)}, f32[]{:T(128)}) all-reduce(f32[5,384]{1,0:T(8,128)S(1)} %get-tuple-element.137, f32[]{:T(128)S(6)} %convert_element_type.78), channel_id=1, replica_groups=mesh['tok'=8,'own'=4] {'tok','own'}, use_global_device_ids=true, to_apply=%region_6.0 | all-reduce | flops 1921 | bytes 15368 | tf_op jit(solution)/shard_map/psum | solution.py:38
  222.1 6.1 %reduce-scatter.2.cloned.1.call-done = f32[4,96,384]{2,1,0:T(8,128)} async-done(((f32[4,384,384]{2,1,0:T(8,128)}), f32[4,96,384]{2,1,0:T(8,128)}) %reduce-scatter.2.cloned.1.call-update) | async-done | bytes 589840 | tf_op jit(solution)/shard_map/reduce_scatter | solution.py:41
  228.4 57.6 %all-reduce.3.cloned.1.call-done = f32[4,96,384]{2,1,0:T(8,128)} async-done(((f32[4,96,384]{2,1,0:T(8,128)}), f32[4,96,384]{2,1,0:T(8,128)}) %all-reduce.3.cloned.1.call-update) | async-done | bytes 589840 | tf_op jit(solution)/shard_map/psum | solution.py:42
  (133 shorter events, 88.1 us)
Async XLA Ops:
  6.5 221.7 %reduce-scatter.2.cloned.1.call-start = ((), (), s32[]{:S(2)}) async-start(), calls=%async_computation.1 | async-start | bytes 2949120 | tf_op jit(solution)/shard_map/reduce_scatter | solution.py:41
  176.6 109.3 %all-reduce.3.cloned.1.call-start = ((), (), s32[]{:S(2)}) async-start(), calls=%async_computation.2 | async-start | bytes 1179648 | tf_op jit(solution)/shard_map/psum | solution.py:42
Sparse Core Ops, SparseCore 0:
  176.7 51.4 reduce-scatter.1
  231.4 54.5 all-reduce.2
where the time goes:
time: 297 us; the launch traced here: 295 us
  other arithmetic  77.5 us (26%)
  matrix products  66.1 us (22%)
  waiting for transfers between devices  63.7 us (21%)
  blocking collectives  44.8 us (15%)
  local copies, waits for them, and re-layouts  28.1 us (9%)
  between operations  14.1 us (5%)
    dot_general x16, matrix products, one_block(): jnp.einsum('ltx,lty->lxy', hot[:-1], hot[1:], preferred_element_type=jnp....  66.1 us
    reduce_sum x16, other arithmetic, one_block(): counts = counts + jnp.sum(hot, axis=1, dtype=jnp.float32)  64.3 us
    psum x1, waiting for transfers between devices, shards(): mine = lax.psum(partial_rows, 'tok')  57.6 us
    psum x1, blocking collectives, shards(): lax.psum((counts, limit.astype(jnp.float32)), ('tok', 'own'))  44.8 us
    slice x16, local copies, waits for them, and re-layouts, one_block(): hot = hot + (piece[:, slot, :, None] == columns).astype(jnp.bfloat16)  27.6 us
    convert_element_type x16, other arithmetic, one_block(): alive = (rows < limit).astype(jnp.bfloat16)  10.4 us
    reduce_scatter x1, waiting for transfers between devices, shards(): lax.psum_scatter(tiles, 'own', scatter_dimension=1, tiled=True)  6.12 us
  transfers between devices with their start and end apart: 2, of which 2 were waited for; matrix products, arithmetic and copies ran while one was open for 0% of the time, Pallas kernels for 0%

commit v1 on v0

v1 whole, which is shorter than its diff:
```python
import functools

import jax
import jax.numpy as jnp
from jax import lax
from jax.experimental import pallas as pl
from jax.experimental.pallas import tpu as pltpu
from jax.sharding import PartitionSpec as P

E = 384
LANES = 128
ROWS = 8
COLS = E // LANES
WORDS = E // 32
HOT = jnp.bfloat16
MESH = pl.DeviceIdType.MESH


def halvings(bits, tiles):
    kept = []
    for _ in range(bits):
        split = tiles % 2 == 0 and (tiles // 2) % COLS == 0
        tiles = tiles // 2 if split else tiles
        kept.append((tiles, split))
    return kept


def kernel(bits, owners, kept, limit_ref, ids_ref, out_ref, hot, macc, acc, first, *rest):
    nst = len(kept)
    stage_in = rest[:nst]
    zsend, zrecv, gathered, csem, ssem, zsem, gsem = rest[nst:]
    layers, chosen, slots = ids_ref.shape
    pairs = layers - 1
    nslot = pairs // 2
    share = acc.shape[2]
    piece = kept[-1][0] if kept else share
    pieces = share // piece

    tok = lax.axis_index("tok")
    own = lax.axis_index("own")
    core = tok % 2
    bit = []
    delta = []
    for i in range(nst):
        bit.append((tok // (2 << i)) % 2)
        delta.append((1 - 2 * bit[i]) * (2 << i))
    if nst >= 2:
        b0, b1, d0, d1 = bit[0], bit[1], delta[0], delta[1]
        bit[0] = b0 * (1 - core) + b1 * core
        bit[1] = b1 * (1 - core) + b0 * core
        delta[0] = d0 * (1 - core) + d1 * core
        delta[1] = d1 * (1 - core) + d0 * core
    partner = [tok + d for d in delta]
    mate = tok + 1 - 2 * core

    barrier = pltpu.get_barrier_semaphore()
    for other in [mate] + partner:
        pl.semaphore_signal(barrier, inc=1, device_id={"tok": other}, device_id_type=MESH)
    for d in range(1, owners):
        pl.semaphore_signal(
            barrier, inc=1, device_id={"own": (own + d) % owners}, device_id_type=MESH
        )

    limit = limit_ref[0]
    step = 512
    row = lax.broadcasted_iota(jnp.int32, (32, step), 0)
    mask = jnp.left_shift(jnp.int32(1), row)

    def build(layer):
        def chunk(index, _):
            start = pl.multiple_of(index * step, step)
            x = ids_ref[layer, :, pl.ds(start, step)]
            at = start + lax.broadcasted_iota(jnp.int32, x.shape, 1)
            high = jnp.where(at < limit, jnp.right_shift(x, 5), WORDS)
            value = jnp.left_shift(jnp.int32(1), jnp.bitwise_and(x, 31))
            for w in range(WORDS):
                word = jnp.sum(jnp.where(high == w, value, 0), axis=0, keepdims=True)
                on = jnp.bitwise_and(jnp.broadcast_to(word, mask.shape), mask) != 0
                hot[layer, pl.ds(32 * w, 32), pl.ds(start, step)] = jnp.where(
                    on, 1.0, 0.0
                ).astype(HOT)
            return 0

        lax.fori_loop(0, slots // step, chunk, 0)

    depth = 1024

    def matmul(pair):
        macc[...] = jnp.zeros_like(macc)

        def chunk(index, _):
            at = pl.ds(pl.multiple_of(index * depth, depth), depth)
            macc[...] += lax.dot_general(
                hot[pair, :, at],
                hot[pair + 1, :, at],
                (((1,), (1,)), ((), ())),
                preferred_element_type=jnp.float32,
            )
            return 0

        lax.fori_loop(0, slots // depth, chunk, 0)
        groups = share // COLS
        for g in range(E // ROWS):
            for b in range(COLS):
                acc[pair, g // groups, (g % groups) * COLS + b] = macc[
                    g * ROWS : (g + 1) * ROWS, b * LANES : (b + 1) * LANES
                ]

    def mine(s):
        return 2 * s + core

    def theirs(s):
        return 2 * s + 1 - core

    def core_copy(s):
        return pltpu.make_async_remote_copy(
            src_ref=acc.at[theirs(s)],
            dst_ref=first.at[s],
            send_sem=csem.at[0, s],
            recv_sem=csem.at[1, s],
            device_id={"tok": mate},
            device_id_type=MESH,
        )

    def offset(i):
        at = 0
        for j in range(i):
            if kept[j][1]:
                at = at + bit[j] * kept[j][0]
        return at

    def stage_copy(s, i):
        size, split = kept[i]
        at = offset(i) + ((1 - bit[i]) * size if split else 0)
        return pltpu.make_async_remote_copy(
            src_ref=acc.at[mine(s), :, pl.ds(at, size)],
            dst_ref=stage_in[i].at[s],
            send_sem=ssem.at[0, s, i],
            recv_sem=ssem.at[1, s, i],
            device_id={"tok": partner[i]},
            device_id_type=MESH,
        )

    def stage_add(s, i):
        size = kept[i][0]
        at = pl.ds(offset(i + 1), size)
        for o in range(owners):
            acc[mine(s), o, at] = acc[mine(s), o, at] + stage_in[i][s, o]

    def z_copy(s, d):
        return pltpu.make_async_remote_copy(
            src_ref=zsend.at[s, (own + d) % owners],
            dst_ref=zrecv.at[s, d - 1],
            send_sem=zsem.at[0, s, d],
            recv_sem=zsem.at[1, s, d],
            device_id={"own": (own + d) % owners},
            device_id_type=MESH,
        )

    def z_send(s):
        at = pl.ds(offset(nst), piece)
        part = acc[mine(s), :, at]
        sums = []
        for b in range(COLS):
            total = jnp.zeros((ROWS, LANES), jnp.float32)
            for o in range(owners):
                for t in range(b, piece, COLS):
                    total = total + part[o, t]
            sums.append(jnp.sum(total, axis=0, keepdims=True))
        sums.append(jnp.zeros((ROWS - COLS, LANES), jnp.float32))
        extra = jnp.concatenate(sums, axis=0)
        for o in range(owners):
            zsend[s, o, pl.ds(0, piece)] = part[o]
            zsend[s, o, piece] = extra
        for d in range(1, owners):
            z_copy(s, d).start()

    def place(i):
        at, span = 0, pieces
        for j in range(i + 1):
            if kept[j][1]:
                span = span // 2
                at = at + bit[j] * span
        return at, span

    def z_sum(s):
        total = zsend[s, own]
        for d in range(1, owners):
            total = total + zrecv[s, d - 1]
        where, _ = place(nst - 1)
        gathered[mine(s), where] = total

    def gather_copy(s, i):
        at, span = place(i)
        there = gathered.at[mine(s), pl.ds(at, span)]
        return pltpu.make_async_remote_copy(
            src_ref=there,
            dst_ref=there,
            send_sem=gsem.at[0, s, i + 1],
            recv_sem=gsem.at[1, s, i + 1],
            device_id={"tok": partner[i]},
            device_id_type=MESH,
        )

    def mate_copy(s):
        return pltpu.make_async_remote_copy(
            src_ref=gathered.at[mine(s)],
            dst_ref=gathered.at[mine(s)],
            send_sem=gsem.at[0, s, 0],
            recv_sem=gsem.at[1, s, 0],
            device_id={"tok": mate},
            device_id_type=MESH,
        )

    def lift(pair):
        second = jnp.zeros((ROWS, LANES), jnp.float32)
        for q in range(pieces):
            second = second + gathered[pair, q, piece]
        second = second / chosen
        total = jnp.sum(jnp.sum(second, axis=1, keepdims=True), axis=0, keepdims=True) / chosen
        for g in range(share // COLS):
            tiles = []
            for b in range(COLS):
                t = g * COLS + b
                tiles.append(gathered[pair, t // piece, t % piece])
            mass = jnp.sum(tiles[0] + tiles[1] + tiles[2], axis=1, keepdims=True) / chosen
            for b in range(COLS):
                product = mass * second[b : b + 1, :]
                out_ref[pair, pl.ds(g * ROWS, ROWS), pl.ds(b * LANES, LANES)] = (
                    tiles[b] * total / jnp.maximum(product, 1.0)
                )

    gathers = [i for i in reversed(range(nst)) if kept[i][1]]

    def stages(s):
        core_copy(s).wait()
        acc[mine(s)] = acc[mine(s)] + first[s]
        for i in range(nst):
            stage_copy(s, i).start()
            yield
            stage_copy(s, i).wait()
            stage_add(s, i)
        z_send(s)
        yield
        for d in range(1, owners):
            z_copy(s, d).wait()
        z_sum(s)
        for i in gathers:
            gather_copy(s, i).start()
            yield
            gather_copy(s, i).wait()
        mate_copy(s).start()
        yield
        mate_copy(s).wait()
        lift(2 * s)
        lift(2 * s + 1)

    def advance(run):
        try:
            next(run)
            return True
        except StopIteration:
            return False

    build(0)
    build(1)
    build(2)
    pl.semaphore_wait(barrier, 1 + nst + owners - 1)
    matmul(theirs(0))
    core_copy(0).start()
    matmul(mine(0))
    runs = [stages(0)]
    advance(runs[0])
    for s in range(1, nslot):
        build(2 * s + 1)
        advance(runs[-1])
        build(2 * s + 2)
        advance(runs[-1])
        matmul(theirs(s))
        core_copy(s).start()
        advance(runs[-1])
        matmul(mine(s))
        runs.append(stages(s))
        advance(runs[-1])
    live = list(runs)
    while live:
        live = [run for run in live if advance(run)]


def shards(expert_ids, shard_length):
    layers, chosen, slots = expert_ids.shape
    toks = lax.axis_size("tok")
    owners = lax.axis_size("own")
    bits = toks.bit_length() - 2
    share = E // owners // ROWS * COLS
    kept = halvings(bits, share)
    piece = kept[-1][0]
    pieces = share // piece
    pairs = layers - 1
    nslot = pairs // 2
    tile = (ROWS, LANES)
    f32 = jnp.float32
    dma = pltpu.SemaphoreType.DMA
    scratch = [
        pltpu.VMEM((layers, E, slots), HOT),
        pltpu.VMEM((E, E), f32),
        pltpu.VMEM((pairs, owners, share) + tile, f32),
        pltpu.VMEM((nslot, owners, share) + tile, f32),
    ]
    scratch += [pltpu.VMEM((nslot, owners, size) + tile, f32) for size, _ in kept]
    scratch += [
        pltpu.VMEM((nslot, owners, piece + 1) + tile, f32),
        pltpu.VMEM((nslot, owners - 1, piece + 1) + tile, f32),
        pltpu.VMEM((pairs, pieces, piece + 1) + tile, f32),
        dma((2, nslot)),
        dma((2, nslot, bits)),
        dma((2, nslot, owners)),
        dma((2, nslot, bits + 1)),
    ]
    return pl.pallas_call(
        functools.partial(kernel, bits, owners, kept),
        out_shape=jax.ShapeDtypeStruct((pairs, E // owners, E), f32),
        in_specs=[
            pl.BlockSpec(memory_space=pltpu.SMEM),
            pl.BlockSpec(memory_space=pltpu.VMEM),
        ],
        out_specs=pl.BlockSpec(memory_space=pltpu.VMEM),
        scratch_shapes=scratch,
        compiler_params=pltpu.CompilerParams(
            collective_id=0, has_side_effects=True, vmem_limit_bytes=60 * 2**20
        ),
    )(shard_length, expert_ids)


def solution(mesh):
    placed = (P(None, None, ("tok", "own")), P(("tok", "own")))
    return jax.shard_map(
        shards, mesh=mesh, in_specs=placed, out_specs=P(None, "own", None), check_vma=False
    )
```

time: 297 us -> 67.8 us (0.23)
  other arithmetic: 77.5 us -> 0 us
  matrix products: 66.1 us -> 0 us
  Pallas kernels: 0 us -> 65 us
  waiting for transfers between devices: 63.7 us -> 0 us
  blocking collectives: 44.8 us -> 0 us
  local copies, waits for them, and re-layouts: 28.1 us -> 1.92 us
  between operations: 14.1 us -> 0.66 us
    dot_general x16 -> x0, matrix products: 66.1 us -> none  [one_block(): jnp.einsum('ltx,lty->lxy', hot[:-1], hot[1:], preferred_element_type=jnp....]
    pallas_call x0 -> x1, Pallas kernels: none -> 65 us  [shards(): pl.pallas_call(functools.partial(kernel, bits, owners, kept), out_shape=j...]
    reduce_sum x16 -> x0, other arithmetic: 64.3 us -> none  [one_block(): counts = counts + jnp.sum(hot, axis=1, dtype=jnp.float32)]
    psum x1 -> x0, waiting for transfers between devices: 57.6 us -> none  [shards(): mine = lax.psum(partial_rows, 'tok')]
    psum x1 -> x0, blocking collectives: 44.8 us -> none  [shards(): lax.psum((counts, limit.astype(jnp.float32)), ('tok', 'own'))]
    slice x17 -> x0, local copies, waits for them, and re-layouts: 27.6 us -> none  [the longest x16 27.6 us: one_block(): hot = hot + (piece[:, slot, :, None] == columns).astype(jnp.bfloat16)]
    convert_element_type x16 -> x0, other arithmetic: 10.4 us -> none  [one_block(): alive = (rows < limit).astype(jnp.bfloat16)]
    reduce_scatter x1 -> x0, waiting for transfers between devices: 6.12 us -> none  [shards(): lax.psum_scatter(tiles, 'own', scatter_dimension=1, tiled=True)]
  transfers between devices with their start and end apart: 2 -> 0, of which waited for: 2 -> 0; matrix products, arithmetic and copies ran while one was open for 0% -> 0% of each run, Pallas kernels for 0% -> 0%
where the time goes in v1:
time: 67.8 us; the launch traced here: 67.6 us
  Pallas kernels  65 us (96%)
  local copies, waits for them, and re-layouts  1.92 us (3%)
    pallas_call x1, Pallas kernels, shards(): pl.pallas_call(functools.partial(kernel, bits, owners, kept), out_shape=j...  65 us
    unnamed x1, local copies, waits for them, and re-layouts  1.92 us

profile of v1, /device:TPU:0, one launch (start us, length us, event | category | flops | bytes accessed | tf_op | source)
XLA Modules:
  0.0 67.6 jit_solution(6142221312663430550)
XLA Ops:
  0.7 65.0 %shard_map.28 = f32[4,96,384]{2,1,0:T(8,128)} custom-call(s32[1]{0:T(128)S(6)} %copy.4.limit_ref, s32[5,8,8192]{2,1,0:T(8,128)} %ids_ref.1), custom_call_target="tpu_custom_call" | custom-call | tf_op jit(solution)/shard_map/pallas_call | solution.py:320
  65.7 1.9 %copy.5 = f32[4,96,384]{2,1,0:T(8,128)} copy(f32[4,96,384]{2,1,0:T(8,128)} %shard_map.28) | data formatting | bytes 1179648

commit v2 on v1

--- a/solution.py
+++ b/solution.py
@@ -12,7 +12,7 @@
 ROWS = 8
 COLS = E // LANES
 WORDS = E // 32
-HOT = jnp.bfloat16
+HOT = jnp.float8_e4m3fn
 MESH = pl.DeviceIdType.MESH
 
 
@@ -25,11 +25,12 @@
     return kept
 
 
-def kernel(bits, owners, kept, limit_ref, ids_ref, out_ref, hot, macc, acc, first, *rest):
+def kernel(bits, owners, kept, limit_ref, ids_ref, out_ref, *rest):
+    layers, chosen, slots = ids_ref.shape
+    hot, (macc, acc, first), rest = rest[:layers], rest[layers : layers + 3], rest[layers + 3 :]
     nst = len(kept)
     stage_in = rest[:nst]
     zsend, zrecv, gathered, csem, ssem, zsem, gsem = rest[nst:]
-    layers, chosen, slots = ids_ref.shape
     pairs = layers - 1
     nslot = pairs // 2
     share = acc.shape[2]
@@ -64,47 +65,53 @@
     limit = limit_ref[0]
     step = 512
     row = lax.broadcasted_iota(jnp.int32, (32, step), 0)
-    mask = jnp.left_shift(jnp.int32(1), row)
-
-    def build(layer):
+    mask = jnp.left_shift(jnp.int32(1), row % 8).astype(jnp.int8)
+
+    def build(layer, start):
+        x = ids_ref[layer, :, pl.ds(start, step)]
+        at = start + lax.broadcasted_iota(jnp.int32, x.shape, 1)
+        high = jnp.where(at < limit, jnp.right_shift(x, 5), WORDS)
+        value = jnp.left_shift(jnp.int32(1), jnp.bitwise_and(x, 31))
+        for w in range(WORDS):
+            word = jnp.sum(jnp.where(high == w, value, 0), axis=0, keepdims=True)
+            bytes4 = jnp.concatenate(
+                [jnp.broadcast_to(jnp.right_shift(word, 8 * j), (8, step)) for j in range(4)],
+                axis=0,
+            ).astype(jnp.int8)
+            on = jnp.bitwise_and(bytes4, mask) != 0
+            hot[layer][pl.ds(32 * w, 32), pl.ds(start, step)] = jnp.where(
+                on, jnp.ones((32, step), HOT), jnp.zeros((32, step), HOT)
+            )
+
+    depth = min(slots, 2048)
+    groups = share // COLS
+
+    def work(layers_now, pair):
+        if pair is not None:
+            macc[...] = jnp.zeros_like(macc)
+
         def chunk(index, _):
-            start = pl.multiple_of(index * step, step)
-            x = ids_ref[layer, :, pl.ds(start, step)]
-            at = start + lax.broadcasted_iota(jnp.int32, x.shape, 1)
-            high = jnp.where(at < limit, jnp.right_shift(x, 5), WORDS)
-            value = jnp.left_shift(jnp.int32(1), jnp.bitwise_and(x, 31))
-            for w in range(WORDS):
-                word = jnp.sum(jnp.where(high == w, value, 0), axis=0, keepdims=True)
-                on = jnp.bitwise_and(jnp.broadcast_to(word, mask.shape), mask) != 0
-                hot[layer, pl.ds(32 * w, 32), pl.ds(start, step)] = jnp.where(
-                    on, 1.0, 0.0
-                ).astype(HOT)
+            start = pl.multiple_of(index * depth, depth)
+            if pair is not None:
+                at = pl.ds(start, depth)
+                macc[...] += lax.dot_general(
+                    hot[pair][:, at],
+                    hot[pair + 1][:, at],
+                    (((1,), (1,)), ((), ())),
+                    preferred_element_type=jnp.float32,
+                )
+            for layer in layers_now:
+                for piece_at in range(0, depth, step):
+                    build(layer, start + piece_at)
             return 0
 
-        lax.fori_loop(0, slots // step, chunk, 0)
-
-    depth = 1024
-
-    def matmul(pair):
-        macc[...] = jnp.zeros_like(macc)
-
-        def chunk(index, _):
-            at = pl.ds(pl.multiple_of(index * depth, depth), depth)
-            macc[...] += lax.dot_general(
-                hot[pair, :, at],
-                hot[pair + 1, :, at],
-                (((1,), (1,)), ((), ())),
-                preferred_element_type=jnp.float32,
-            )
-            return 0
-
         lax.fori_loop(0, slots // depth, chunk, 0)
-        groups = share // COLS
-        for g in range(E // ROWS):
-            for b in range(COLS):
-                acc[pair, g // groups, (g % groups) * COLS + b] = macc[
-                    g * ROWS : (g + 1) * ROWS, b * LANES : (b + 1) * LANES
-                ]
+        if pair is not None:
+            for g in range(E // ROWS):
+                for b in range(COLS):
+                    acc[pair, g // groups, (g % groups) * COLS + b] = macc[
+                        g * ROWS : (g + 1) * ROWS, b * LANES : (b + 1) * LANES
+                    ]
 
     def mine(s):
         return 2 * s + core
@@ -262,26 +269,19 @@
         except StopIteration:
             return False
 
-    build(0)
-    build(1)
-    build(2)
-    pl.semaphore_wait(barrier, 1 + nst + owners - 1)
-    matmul(theirs(0))
-    core_copy(0).start()
-    matmul(mine(0))
-    runs = [stages(0)]
-    advance(runs[0])
-    for s in range(1, nslot):
-        build(2 * s + 1)
-        advance(runs[-1])
-        build(2 * s + 2)
-        advance(runs[-1])
-        matmul(theirs(s))
-        core_copy(s).start()
-        advance(runs[-1])
-        matmul(mine(s))
-        runs.append(stages(s))
-        advance(runs[-1])
+    work((0,), None)
+    work((1,), None)
+    runs = []
+    for p in range(pairs):
+        work((p + 2,) if p + 2 < layers else (), p)
+        if p == 0:
+            pl.semaphore_wait(barrier, 1 + nst + owners - 1)
+        for run in runs:
+            advance(run)
+        if p % 2 == 1:
+            core_copy(p // 2).start()
+            runs.append(stages(p // 2))
+            advance(runs[-1])
     live = list(runs)
     while live:
         live = [run for run in live if advance(run)]
@@ -301,8 +301,8 @@
     tile = (ROWS, LANES)
     f32 = jnp.float32
     dma = pltpu.SemaphoreType.DMA
-    scratch = [
-        pltpu.VMEM((layers, E, slots), HOT),
+    scratch = [pltpu.VMEM((E, slots), HOT)] * layers
+    scratch += [
         pltpu.VMEM((E, E), f32),
         pltpu.VMEM((pairs, owners, share) + tile, f32),
         pltpu.VMEM((nslot, owners, share) + tile, f32),

time: 67.8 us -> 55.5 us (0.82)
  Pallas kernels: 65 us -> 52.8 us
    pallas_call x1, Pallas kernels: 65 us -> 52.8 us  [shards(): pl.pallas_call(functools.partial(kernel, bits, owners, kept), out_shape=j...]
where the time goes in v2:
time: 55.5 us; the launch traced here: 55.3 us
  Pallas kernels  52.8 us (95%)
  local copies, waits for them, and re-layouts  1.92 us (3%)
  between operations  0.66 us (1%)
    pallas_call x1, Pallas kernels, shards(): pl.pallas_call(functools.partial(kernel, bits, owners, kept), out_shape=j...  52.8 us
    unnamed x1, local copies, waits for them, and re-layouts  1.92 us

profile of v2, /device:TPU:0, one launch (start us, length us, event | category | flops | bytes accessed | tf_op | source)
XLA Modules:
  0.0 55.3 jit_solution(11939299904285977629)
XLA Ops:
  0.7 52.8 %shard_map.28 = f32[4,96,384]{2,1,0:T(8,128)} custom-call(s32[1]{0:T(128)S(6)} %copy.4.limit_ref, s32[5,8,8192]{2,1,0:T(8,128)} %ids_ref.1), custom_call_target="tpu_custom_call" | custom-call | tf_op jit(solution)/shard_map/pallas_call | solution.py:320
  53.4 1.9 %copy.5 = f32[4,96,384]{2,1,0:T(8,128)} copy(f32[4,96,384]{2,1,0:T(8,128)} %shard_map.28) | data formatting | bytes 1179648

commit v3 on v2

--- a/solution.py
+++ b/solution.py
@@ -30,7 +30,8 @@
     hot, (macc, acc, first), rest = rest[:layers], rest[layers : layers + 3], rest[layers + 3 :]
     nst = len(kept)
     stage_in = rest[:nst]
-    zsend, zrecv, gathered, csem, ssem, zsem, gsem = rest[nst:]
+    zsend, zrecv, gathered, xsum, xin, xz, xcol = rest[nst : nst + 7]
+    csem, ssem, zsem, gsem, xsem, xzsem = rest[nst + 7 :]
     pairs = layers - 1
     nslot = pairs // 2
     share = acc.shape[2]
@@ -54,13 +55,24 @@
     partner = [tok + d for d in delta]
     mate = tok + 1 - 2 * core
 
+    split = [i for i in range(nst) if kept[i][1]]
+    peers = {}
+    for code in range(1, 2 ** len(split)):
+        peers[code] = tok + sum(delta[i] for n, i in enumerate(split) if (code >> n) % 2)
+    greet = [mate] + list(peers.values())
+    greet += [partner[i] for i in range(nst) if i not in split]
+
     barrier = pltpu.get_barrier_semaphore()
-    for other in [mate] + partner:
+    for other in greet:
         pl.semaphore_signal(barrier, inc=1, device_id={"tok": other}, device_id_type=MESH)
     for d in range(1, owners):
         pl.semaphore_signal(
             barrier, inc=1, device_id={"own": (own + d) % owners}, device_id_type=MESH
         )
+    turn = sorted(range(1, owners), key=lambda d: -min(d, owners - d)) + [0]
+
+    def to(d):
+        return (own + d) % owners
 
     limit = limit_ref[0]
     step = 512
@@ -119,12 +131,12 @@
     def theirs(s):
         return 2 * s + 1 - core
 
-    def core_copy(s):
-        return pltpu.make_async_remote_copy(
-            src_ref=acc.at[theirs(s)],
-            dst_ref=first.at[s],
-            send_sem=csem.at[0, s],
-            recv_sem=csem.at[1, s],
+    def core_copy(s, d):
+        return pltpu.make_async_remote_copy(
+            src_ref=acc.at[theirs(s), to(d)],
+            dst_ref=first.at[s, to(d)],
+            send_sem=csem.at[0, s, d],
+            recv_sem=csem.at[1, s, d],
             device_id={"tok": mate},
             device_id_type=MESH,
         )
@@ -136,94 +148,105 @@
                 at = at + bit[j] * kept[j][0]
         return at
 
-    def stage_copy(s, i):
-        size, split = kept[i]
-        at = offset(i) + ((1 - bit[i]) * size if split else 0)
-        return pltpu.make_async_remote_copy(
-            src_ref=acc.at[mine(s), :, pl.ds(at, size)],
-            dst_ref=stage_in[i].at[s],
-            send_sem=ssem.at[0, s, i],
-            recv_sem=ssem.at[1, s, i],
+    def stage_copy(s, i, d):
+        size, halves = kept[i]
+        at = offset(i) + ((1 - bit[i]) * size if halves else 0)
+        return pltpu.make_async_remote_copy(
+            src_ref=acc.at[mine(s), to(d), pl.ds(at, size)],
+            dst_ref=stage_in[i].at[s, to(d)],
+            send_sem=ssem.at[0, s, i, d],
+            recv_sem=ssem.at[1, s, i, d],
             device_id={"tok": partner[i]},
             device_id_type=MESH,
         )
 
-    def stage_add(s, i):
-        size = kept[i][0]
-        at = pl.ds(offset(i + 1), size)
-        for o in range(owners):
-            acc[mine(s), o, at] = acc[mine(s), o, at] + stage_in[i][s, o]
+    def stage_add(s, i, d):
+        at = pl.ds(offset(i + 1), kept[i][0])
+        acc[mine(s), to(d), at] = acc[mine(s), to(d), at] + stage_in[i][s, to(d)]
 
     def z_copy(s, d):
         return pltpu.make_async_remote_copy(
-            src_ref=zsend.at[s, (own + d) % owners],
+            src_ref=zsend.at[s, d],
             dst_ref=zrecv.at[s, d - 1],
             send_sem=zsem.at[0, s, d],
             recv_sem=zsem.at[1, s, d],
-            device_id={"own": (own + d) % owners},
-            device_id_type=MESH,
-        )
-
-    def z_send(s):
-        at = pl.ds(offset(nst), piece)
-        part = acc[mine(s), :, at]
+            device_id={"own": to(d)},
+            device_id_type=MESH,
+        )
+
+    def column_sums(s):
         sums = []
         for b in range(COLS):
             total = jnp.zeros((ROWS, LANES), jnp.float32)
             for o in range(owners):
-                for t in range(b, piece, COLS):
-                    total = total + part[o, t]
+                for t in range(b, share, COLS):
+                    total = total + acc[mine(s), o, t]
             sums.append(jnp.sum(total, axis=0, keepdims=True))
         sums.append(jnp.zeros((ROWS - COLS, LANES), jnp.float32))
-        extra = jnp.concatenate(sums, axis=0)
-        for o in range(owners):
-            zsend[s, o, pl.ds(0, piece)] = part[o]
-            zsend[s, o, piece] = extra
-        for d in range(1, owners):
-            z_copy(s, d).start()
-
-    def place(i):
+        return jnp.concatenate(sums, axis=0)
+
+    def sums_copy(s, i):
+        return pltpu.make_async_remote_copy(
+            src_ref=xsum.at[s, i],
+            dst_ref=xin.at[s, i],
+            send_sem=xsem.at[0, s, i],
+            recv_sem=xsem.at[1, s, i],
+            device_id={"tok": partner[i]},
+            device_id_type=MESH,
+        )
+
+    def sums_z_copy(s, d):
+        return pltpu.make_async_remote_copy(
+            src_ref=xsum.at[s, nst],
+            dst_ref=xz.at[s, d - 1],
+            send_sem=xzsem.at[0, s, d],
+            recv_sem=xzsem.at[1, s, d],
+            device_id={"own": to(d)},
+            device_id_type=MESH,
+        )
+
+    def sums_mate_copy(s):
+        return pltpu.make_async_remote_copy(
+            src_ref=xcol.at[mine(s)],
+            dst_ref=xcol.at[mine(s)],
+            send_sem=xzsem.at[0, s, 0],
+            recv_sem=xzsem.at[1, s, 0],
+            device_id={"tok": mate},
+            device_id_type=MESH,
+        )
+
+    def place(code):
         at, span = 0, pieces
-        for j in range(i + 1):
-            if kept[j][1]:
-                span = span // 2
-                at = at + bit[j] * span
-        return at, span
-
-    def z_sum(s):
-        total = zsend[s, own]
-        for d in range(1, owners):
-            total = total + zrecv[s, d - 1]
-        where, _ = place(nst - 1)
-        gathered[mine(s), where] = total
-
-    def gather_copy(s, i):
-        at, span = place(i)
-        there = gathered.at[mine(s), pl.ds(at, span)]
+        for n, i in enumerate(split):
+            span = span // 2
+            held = 1 - bit[i] if (code >> n) % 2 else bit[i]
+            at = at + held * span
+        return at
+
+    def gather_copy(s, code):
+        there = gathered.at[mine(s), place(0)]
         return pltpu.make_async_remote_copy(
             src_ref=there,
             dst_ref=there,
-            send_sem=gsem.at[0, s, i + 1],
-            recv_sem=gsem.at[1, s, i + 1],
-            device_id={"tok": partner[i]},
-            device_id_type=MESH,
-        )
-
-    def mate_copy(s):
-        return pltpu.make_async_remote_copy(
-            src_ref=gathered.at[mine(s)],
-            dst_ref=gathered.at[mine(s)],
-            send_sem=gsem.at[0, s, 0],
-            recv_sem=gsem.at[1, s, 0],
+            send_sem=gsem.at[0, s, 0, code],
+            recv_sem=gsem.at[1, s, 0, code],
+            device_id={"tok": peers[code]},
+            device_id_type=MESH,
+        )
+
+    def mate_copy(s, code):
+        there = gathered.at[mine(s), place(code)]
+        return pltpu.make_async_remote_copy(
+            src_ref=there,
+            dst_ref=there,
+            send_sem=gsem.at[0, s, 1, code],
+            recv_sem=gsem.at[1, s, 1, code],
             device_id={"tok": mate},
             device_id_type=MESH,
         )
 
     def lift(pair):
-        second = jnp.zeros((ROWS, LANES), jnp.float32)
-        for q in range(pieces):
-            second = second + gathered[pair, q, piece]
-        second = second / chosen
+        second = xcol[pair] / chosen
         total = jnp.sum(jnp.sum(second, axis=1, keepdims=True), axis=0, keepdims=True) / chosen
         for g in range(share // COLS):
             tiles = []
@@ -237,30 +260,55 @@
                     tiles[b] * total / jnp.maximum(product, 1.0)
                 )
 
-    gathers = [i for i in reversed(range(nst)) if kept[i][1]]
-
     def stages(s):
-        core_copy(s).wait()
-        acc[mine(s)] = acc[mine(s)] + first[s]
+        for d in turn:
+            core_copy(s, d).wait()
+            acc[mine(s), to(d)] = acc[mine(s), to(d)] + first[s, to(d)]
+            stage_copy(s, 0, d).start()
+        xsum[s, 0] = column_sums(s)
+        sums_copy(s, 0).start()
+        yield
         for i in range(nst):
-            stage_copy(s, i).start()
+            sums_copy(s, i).wait()
+            xsum[s, i + 1] = xsum[s, i] + xin[s, i]
+            if i + 1 < nst:
+                sums_copy(s, i + 1).start()
+            else:
+                for d in turn[:-1]:
+                    sums_z_copy(s, d).start()
+            for d in turn:
+                stage_copy(s, i, d).wait()
+                stage_add(s, i, d)
+                if i + 1 < nst:
+                    stage_copy(s, i + 1, d).start()
+                    continue
+                zsend[s, d] = acc[mine(s), to(d), pl.ds(offset(nst), piece)]
+                if d:
+                    z_copy(s, d).start()
             yield
-            stage_copy(s, i).wait()
-            stage_add(s, i)
-        z_send(s)
+        column = xsum[s, nst]
+        for d in turn[:-1]:
+            sums_z_copy(s, d).wait()
+            column = column + xz[s, d - 1]
+        xcol[mine(s)] = column
+        sums_mate_copy(s).start()
+        total = zsend[s, 0]
+        for d in turn[:-1]:
+            z_copy(s, d).wait()
+            total = total + zrecv[s, d - 1]
+        gathered[mine(s), place(0)] = total
+        for code in reversed(peers):
+            gather_copy(s, code).start()
+        mate_copy(s, 0).start()
         yield
-        for d in range(1, owners):
-            z_copy(s, d).wait()
-        z_sum(s)
-        for i in gathers:
-            gather_copy(s, i).start()
-            yield
-            gather_copy(s, i).wait()
-        mate_copy(s).start()
-        yield
-        mate_copy(s).wait()
-        lift(2 * s)
-        lift(2 * s + 1)
+        for code in peers:
+            gather_copy(s, code).wait()
+            mate_copy(s, code).start()
+        lift(mine(s))
+        sums_mate_copy(s).wait()
+        for code in [0] + list(peers):
+            mate_copy(s, code).wait()
+        lift(theirs(s))
 
     def advance(run):
         try:
@@ -275,11 +323,12 @@
     for p in range(pairs):
         work((p + 2,) if p + 2 < layers else (), p)
         if p == 0:
-            pl.semaphore_wait(barrier, 1 + nst + owners - 1)
-        for run in runs:
-            advance(run)
+            pl.semaphore_wait(barrier, len(greet) + owners - 1)
         if p % 2 == 1:
-            core_copy(p // 2).start()
+            for d in turn:
+                core_copy(p // 2, d).start()
+            for run in runs:
+                advance(run)
             runs.append(stages(p // 2))
             advance(runs[-1])
     live = list(runs)
@@ -309,13 +358,19 @@
     ]
     scratch += [pltpu.VMEM((nslot, owners, size) + tile, f32) for size, _ in kept]
     scratch += [
-        pltpu.VMEM((nslot, owners, piece + 1) + tile, f32),
-        pltpu.VMEM((nslot, owners - 1, piece + 1) + tile, f32),
-        pltpu.VMEM((pairs, pieces, piece + 1) + tile, f32),
-        dma((2, nslot)),
+        pltpu.VMEM((nslot, owners, piece) + tile, f32),
+        pltpu.VMEM((nslot, owners - 1, piece) + tile, f32),
+        pltpu.VMEM((pairs, pieces, piece) + tile, f32),
+        pltpu.VMEM((nslot, bits + 1) + tile, f32),
+        pltpu.VMEM((nslot, bits) + tile, f32),
+        pltpu.VMEM((nslot, owners - 1) + tile, f32),
+        pltpu.VMEM((pairs,) + tile, f32),
+        dma((2, nslot, owners)),
+        dma((2, nslot, bits, owners)),
+        dma((2, nslot, owners)),
+        dma((2, nslot, 2, pieces)),
         dma((2, nslot, bits)),
         dma((2, nslot, owners)),
-        dma((2, nslot, bits + 1)),
     ]
     return pl.pallas_call(
         functools.partial(kernel, bits, owners, kept),

time: 55.5 us -> 46.2 us (0.83)
  Pallas kernels: 52.8 us -> 43.4 us
    pallas_call x1, Pallas kernels: 52.8 us -> 43.4 us  [shards(): pl.pallas_call(functools.partial(kernel, bits, owners, kept), out_shape=j...]
where the time goes in v3:
time: 46.2 us; the launch traced here: 46 us
  Pallas kernels  43.4 us (94%)
  local copies, waits for them, and re-layouts  1.92 us (4%)
  between operations  0.66 us (1%)
    pallas_call x1, Pallas kernels, shards(): pl.pallas_call(functools.partial(kernel, bits, owners, kept), out_shape=j...  43.4 us
    unnamed x1, local copies, waits for them, and re-layouts  1.92 us

profile of v3, /device:TPU:0, one launch (start us, length us, event | category | flops | bytes accessed | tf_op | source)
XLA Modules:
  0.0 46.0 jit_solution(10097654108884150604)
XLA Ops:
  0.7 43.4 %shard_map.28 = f32[4,96,384]{2,1,0:T(8,128)} custom-call(s32[1]{0:T(128)S(6)} %copy.4.limit_ref, s32[5,8,8192]{2,1,0:T(8,128)} %ids_ref.1), custom_call_target="tpu_custom_call" | custom-call | tf_op jit(solution)/shard_map/pallas_call | solution.py:375
  44.0 1.9 %copy.5 = f32[4,96,384]{2,1,0:T(8,128)} copy(f32[4,96,384]{2,1,0:T(8,128)} %shard_map.28) | data formatting | bytes 1179648

commit v4 on v3

--- a/solution.py
+++ b/solution.py
@@ -327,10 +327,9 @@
         if p % 2 == 1:
             for d in turn:
                 core_copy(p // 2, d).start()
-            for run in runs:
+            runs.append(stages(p // 2))
+            for run in reversed(runs):
                 advance(run)
-            runs.append(stages(p // 2))
-            advance(runs[-1])
     live = list(runs)
     while live:
         live = [run for run in live if advance(run)]

time: 46.2 us -> 47.7 us (1.032)
  Pallas kernels: 43.4 us -> 44.9 us
    pallas_call x1, Pallas kernels: 43.4 us -> 44.9 us  [shards(): pl.pallas_call(functools.partial(kernel, bits, owners, kept), out_shape=j...]
where the time goes in v4:
time: 47.7 us; the launch traced here: 47.5 us
  Pallas kernels  44.9 us (94%)
  local copies, waits for them, and re-layouts  1.92 us (4%)
  between operations  0.66 us (1%)
    pallas_call x1, Pallas kernels, shards(): pl.pallas_call(functools.partial(kernel, bits, owners, kept), out_shape=j...  44.9 us
    unnamed x1, local copies, waits for them, and re-layouts  1.92 us

profile of v4, /device:TPU:0, one launch (start us, length us, event | category | flops | bytes accessed | tf_op | source)
XLA Modules:
  0.0 47.5 jit_solution(11526032724773922982)
XLA Ops:
  0.7 44.9 %shard_map.28 = f32[4,96,384]{2,1,0:T(8,128)} custom-call(s32[1]{0:T(128)S(6)} %copy.4.limit_ref, s32[5,8,8192]{2,1,0:T(8,128)} %ids_ref.1), custom_call_target="tpu_custom_call" | custom-call | tf_op jit(solution)/shard_map/pallas_call | solution.py:374
  45.6 1.9 %copy.5 = f32[4,96,384]{2,1,0:T(8,128)} copy(f32[4,96,384]{2,1,0:T(8,128)} %shard_map.28) | data formatting | bytes 1179648
